TPU v7x, 32 devices: a whole 2x2x4 slice. The times are simulated.
32 devices in a mesh: row: 8 (over y, x, core), col: 4 (over z).
Axes of the slice: x: 2, y: 2, z: 4, core: 2. Of those that a mesh axis runs over, the one named last changes fastest.
Arguments:
- probes: float32 [16384, 256], P(('row', 'col')), may hold values from -6 to 6
- spectrum: float32 [32, 512], P(('row', 'col')), may hold values from 0.5 to 4
Outputs:
- leaf_basis: float32 [16384, 256], P(('row', 'col'))
- leaf_transfer: float32 [8192, 256], P(('row', 'col'))
- pair_transfer: float32 [4096, 256], P(('row', 'col'))
- group_factor: float32 [2048, 256], P(('row', 'col'))
All inputs are finite; a program needn't handle non-finite values.
Results may differ from a plain program's by a relative error of at most 0.000076.
Values sent between devices are 32-bit elements; how exact they have to be, the bound alone decides.
No kernel may reach another device: no remote copies, remote signals or barrier semaphores. Data moves between devices by JAX's collectives and lax.ppermute only.
A program may use at most 64 MiB of HBM per device.

v0:
```python
import math
import jax
import jax.numpy as jnp
from jax import lax
from jax.sharding import PartitionSpec as P


def partner(value, axis, distance):
    mask = 2**distance
    pairs = [(source, source ^ mask) for source in range(lax.axis_size(axis))]
    return lax.ppermute(value, axis, pairs)


def circle(product, length):
    angle = 2.0 * math.pi / length * (product % length).astype(jnp.float32)
    return (jnp.cos(angle), jnp.sin(angle))


def lower_solve(low, rhs):
    return jax.scipy.linalg.solve_triangular(low, rhs, lower=True)


def matmul(left, right):
    return jnp.dot(left, right, precision=lax.Precision.HIGHEST)


def local(probes, spectrum):
    rows_dev, width = probes.shape
    n_row = lax.axis_size("row")
    n_col = lax.axis_size("col")
    devices = n_row * n_col
    slab = rows_dev // devices
    total = rows_dev * devices
    col_index = lax.axis_index("col")
    flat = lax.axis_index("row") * n_col + col_index
    highest = lax.Precision.HIGHEST
    spread = lax.all_to_all(
        probes.reshape(1, rows_dev, width), ("row", "col"), split_axis=1, concat_axis=0, tiled=True
    )
    small_index = jnp.arange(devices, dtype=jnp.int32)
    cos_small, sin_small = circle(small_index[:, None] * small_index[None, :], devices)
    real_first = jnp.einsum("ka,abr->kbr", cos_small, spread, precision=highest)
    imag_first = -jnp.einsum("ka,abr->kbr", sin_small, spread, precision=highest)
    local_rows = flat * slab + jnp.arange(slab, dtype=jnp.int32)
    cos_turn, sin_turn = circle(small_index[:, None] * local_rows[None, :], total)
    cos_turn = cos_turn[:, :, None]
    sin_turn = sin_turn[:, :, None]
    turned = jnp.stack(
        [
            real_first * cos_turn + imag_first * sin_turn,
            imag_first * cos_turn - real_first * sin_turn,
        ]
    )
    columns = lax.all_to_all(turned, ("row", "col"), split_axis=1, concat_axis=2, tiled=True)
    columns = columns.reshape(2, rows_dev, width)
    big_index = jnp.arange(rows_dev, dtype=jnp.int32)
    cos_big, sin_big = circle(big_index[:, None] * big_index[None, :], rows_dev)
    real_col, imag_col = (columns[0], columns[1])
    symbol = spectrum[0][:, None]
    real_spec = (matmul(cos_big, real_col) + matmul(sin_big, imag_col)) * symbol
    imag_spec = (matmul(cos_big, imag_col) - matmul(sin_big, real_col)) * symbol
    real_back = matmul(cos_big, real_spec) - matmul(sin_big, imag_spec)
    imag_back = matmul(cos_big, imag_spec) + matmul(sin_big, real_spec)
    cos_back, sin_back = circle(big_index * flat, total)
    cos_back = cos_back[:, None]
    sin_back = sin_back[:, None]
    returned = jnp.stack(
        [real_back * cos_back - imag_back * sin_back, imag_back * cos_back + real_back * sin_back]
    )
    spectra = lax.all_to_all(
        returned.reshape(2, 1, rows_dev, width),
        ("row", "col"),
        split_axis=2,
        concat_axis=1,
        tiled=True,
    )
    partial_sample = (
        jnp.einsum("ak,kbr->abr", cos_small, spectra[0], precision=highest)
        - jnp.einsum("ak,kbr->abr", sin_small, spectra[1], precision=highest)
    ) / total
    sample = lax.all_to_all(partial_sample, ("row", "col"), split_axis=0, concat_axis=1, tiled=True)
    sample = sample.reshape(rows_dev, width)
    leaf_gram = matmul(sample.T, sample) / rows_dev
    leaf_low = jnp.linalg.cholesky(leaf_gram)
    leaf_basis = lower_solve(leaf_low, sample.T).T
    pair_gram = leaf_gram + partner(leaf_gram, "col", 0)
    group_gram = pair_gram + partner(pair_gram, "col", 1)
    pair_low = jnp.linalg.cholesky(pair_gram)
    leaf_transfer = lower_solve(pair_low, leaf_low).T
    group_low = jnp.linalg.cholesky(group_gram)
    pair_whole = lower_solve(group_low, pair_low).T
    half = width // 2
    pair_transfer = lax.dynamic_slice_in_dim(pair_whole, col_index % 2 * half, half, 0)
    quarter = width // 4
    group_factor = lax.dynamic_slice_in_dim(group_low.T, col_index % 4 * quarter, quarter, 0)
    return (leaf_basis, leaf_transfer, pair_transfer, group_factor)


def solution(mesh):
    placed = (P(("row", "col"), None), P(("row", "col"), None))
    return jax.shard_map(
        local,
        mesh=mesh,
        in_specs=placed,
        out_specs=(
            P(("row", "col"), None),
            P(("row", "col"), None),
            P(("row", "col"), None),
            P(("row", "col"), None),
        ),
        check_vma=False,
    )
```

profile of v0, /device:TPU:0, one launch (start us, length us, event | category | flops | bytes accessed | tf_op | source)
XLA Modules:
  0.0 351.0 jit_solution(7423663234639681763)
XLA Ops:
  2.8 7.3 %all-to-all-start = ((f32[1,512,256]{2,0,1:T(1,128)}), f32[1,512,256]{2,0,1:T(1,128)S(1)}, u32[]{:S(2)}, u32[]{:S(2)}) async-start(f32[1,512,256]{2,0,1:T(1,128)} %reshape.142), calls=%async_computation | async-start | bytes 1048576 | tf_op jit(solution)/shard_map/all_to_all | solution.py:37
  10.3 14.2 %all-to-all-done = f32[1,512,256]{2,0,1:T(1,128)S(1)} async-done(((f32[1,512,256]{2,0,1:T(1,128)}), f32[1,512,256]{2,0,1:T(1,128)S(1)}, u32[]{:S(2)}, u32[]{:S(2)}) %all-to-all-start) | async-done | bytes 524320 | tf_op jit(solution)/shard_map/all_to_all | solution.py:37
  32.5 25.0 %all-to-all-done.1 = f32[2,32,16,256]{3,2,0,1:T(8,128)S(1)} async-done(((f32[2,32,16,256]{3,2,0,1:T(8,128)}), f32[2,32,16,256]{3,2,0,1:T(8,128)S(1)}, u32[]{:S(2)}, u32[]{:S(2)}) %all-to-all-start.1) | async-done | bytes 1048608 | tf_op jit(solution)/shard_map/all_to_all | solution.py:54
  57.6 5.6 %fusion.21 = f32[512,256]{1,0:T(8,128)S(1)} fusion(f32[512,256]{1,0:T(8,128)S(1)} %bitcast.154), kind=kOutput, calls=%fused_computation.45 | convolution fusion | flops 808976384 | bytes 1048576 | tf_op jit(solution)/shard_map/dot_general | solution.py:24
  63.2 5.6 %fusion.17 = f32[512,256]{1,0:T(8,128)S(1)} fusion(f32[512,256]{1,0:T(8,128)S(1)} %bitcast.156), kind=kOutput, calls=%fused_computation.43 | convolution fusion | flops 808976384 | bytes 1048576 | tf_op jit(solution)/shard_map/dot_general | solution.py:24
  68.8 5.6 %fusion = f32[512,256]{1,0:T(8,128)S(1)} fusion(f32[512,256]{1,0:T(8,128)S(1)} %fusion.21, f32[512,256]{1,0:T(8,128)S(1)} %bitcast.157, f32[512]{0:T(512)S(1)} %bitcast.158), kind=kOutput, calls=%fused_computation.13 | convolution fusion | flops 809238528 | bytes 1574912 | tf_op jit(solution)/shard_map/dot_general | solution.py:24
  74.5 5.6 %fusion.1 = f32[512,256]{1,0:T(8,128)S(1)} fusion(f32[512,256]{1,0:T(8,128)S(1)} %fusion.17, f32[512,256]{1,0:T(8,128)S(1)} %bitcast.155, f32[512]{0:T(512)S(1)} %bitcast.159), kind=kOutput, calls=%fused_computation.14 | convolution fusion | flops 809238528 | bytes 1574912 | tf_op jit(solution)/shard_map/dot_general | solution.py:24
  80.1 5.6 %fusion.15 = f32[512,256]{1,0:T(8,128)S(1)} fusion(f32[512,256]{1,0:T(8,128)S(1)} %fusion.1), kind=kOutput, calls=%fused_computation.42 | convolution fusion | flops 808976384 | bytes 1048576 | tf_op jit(solution)/shard_map/dot_general | solution.py:24
  91.4 5.6 %convolution_add_fusion = f32[512,256]{1,0:T(8,128)S(1)} fusion(f32[512,256]{1,0:T(8,128)S(1)} %fusion.15, f32[512,256]{1,0:T(8,128)S(1)} %fusion), kind=kOutput, calls=%fused_computation.9 | convolution fusion | flops 809107456 | bytes 1572864 | tf_op jit(solution)/shard_map/dot_general | solution.py:24
  97.0 7.2 %subtract_bitcast_fusion = (f32[1,512,256]{2,1,0:T(8,128)S(1)}, f32[1,512,256]{2,1,0:T(8,128)S(1)}) fusion(f32[512,256]{1,0:T(8,128)S(1)} %convolution_add_fusion, f32[512]{0:T(512)S(1)} %get-tuple-element.108, f32[512]{0:T(512)S(1)} %get-tuple-element.109, f32[512,256]{1,0:T(8,128)S(1)} %fusion.19, f32[512,256]{1,0:T(8,128)S(1)} %fusion.1), kind=kOutput, calls=%fused_computation.37 | convolution fusion | flops 809893888 | bytes 2625536 | tf_op jit(solution)/shard_map/dot_general | solution.py:24
  105.1 29.7 %all_to_all.19 = f32[2,1,512,256]{3,0,1,2:T(2,128)S(1)} all-to-all(f32[2,1,512,256]{3,0,1,2:T(2,128)S(1)} %copy.57), channel_id=1, replica_groups=mesh['row'=8,'col'=4] {'row','col'}, dimensions={2} | all-to-all | bytes 2097152 | tf_op jit(solution)/shard_map/all_to_all | solution.py:70
  143.1 14.3 %all-to-all-done.3 = f32[32,16,256]{2,1,0:T(8,128)S(1)} async-done(((f32[32,16,256]{2,1,0:T(8,128)}), f32[32,16,256]{2,1,0:T(8,128)S(1)}, u32[]{:S(2)}, u32[]{:S(2)}) %all-to-all-start.3) | async-done | bytes 524320 | tf_op jit(solution)/shard_map/all_to_all | solution.py:81
  161.3 11.7 %cholesky.172 = f32[128,128]{1,0:T(8,128)S(1)} custom-call(f32[128,128]{1,0:T(8,128)S(1)} %cholesky.270), custom_call_target="Cholesky" | custom-call | tf_op jit(solution)/shard_map/jit(cholesky)/cholesky | solution.py:84
  173.0 9.8 %custom-call.19 = f32[1,128,128]{1,2,0:T(8,128)S(1)} custom-call(f32[1,128,128]{2,1,0:T(8,128)S(1)} %get-tuple-element.101), custom_call_target="InvertDiagBlocksLowerTriangular" | custom-call | tf_op jit(solution)/shard_map/jit(cholesky)/cholesky | solution.py:84
  183.3 11.7 %cholesky.189 = f32[128,128]{1,0:T(8,128)S(1)} custom-call(f32[128,128]{1,0:T(8,128)S(1)} %convolution_subtract_fusion.6), custom_call_target="Cholesky" | custom-call | tf_op jit(solution)/shard_map/jit(cholesky)/cholesky | solution.py:84
  201.8 19.8 %custom-call.15 = f32[2,128,128]{1,2,0:T(8,128)S(1)} custom-call(f32[2,128,128]{2,1,0:T(8,128)S(1)} %get-tuple-element.21), custom_call_target="InvertDiagBlocksLowerTriangular" | custom-call | tf_op jit(solution)/shard_map/jit(_solve_triangular)/triangular_solve | solution.py:20
  225.3 11.7 %cholesky.206 = f32[128,128]{1,0:T(8,128)S(1)} custom-call(f32[128,128]{1,0:T(8,128)S(1)} %cholesky.273), custom_call_target="Cholesky" | custom-call | tf_op jit(solution)/shard_map/jit(cholesky)/cholesky | solution.py:88
  237.0 9.8 %custom-call.20 = f32[1,128,128]{1,2,0:T(8,128)S(1)} custom-call(f32[1,128,128]{2,1,0:T(8,128)S(1)} %get-tuple-element.97), custom_call_target="InvertDiagBlocksLowerTriangular" | custom-call | tf_op jit(solution)/shard_map/jit(cholesky)/cholesky | solution.py:88
  247.3 11.7 %cholesky.223 = f32[128,128]{1,0:T(8,128)S(1)} custom-call(f32[128,128]{1,0:T(8,128)S(1)} %slice_subtract_fusion.1), custom_call_target="Cholesky" | custom-call | tf_op jit(solution)/shard_map/jit(cholesky)/cholesky | solution.py:88
  265.7 19.9 %custom-call.21 = f32[2,128,128]{1,2,0:T(8,128)S(1)} custom-call(f32[2,128,128]{2,1,0:T(8,128)S(1)} %get-tuple-element.28), custom_call_target="InvertDiagBlocksLowerTriangular" | custom-call | tf_op jit(solution)/shard_map/jit(_solve_triangular)/triangular_solve | solution.py:20
  287.6 11.7 %cholesky.240 = f32[128,128]{1,0:T(8,128)S(1)} custom-call(f32[128,128]{1,0:T(8,128)S(1)} %cholesky.276), custom_call_target="Cholesky" | custom-call | tf_op jit(solution)/shard_map/jit(cholesky)/cholesky | solution.py:90
  299.4 9.8 %custom-call.22 = f32[1,128,128]{1,2,0:T(8,128)S(1)} custom-call(f32[1,128,128]{2,1,0:T(8,128)S(1)} %get-tuple-element.93), custom_call_target="InvertDiagBlocksLowerTriangular" | custom-call | tf_op jit(solution)/shard_map/jit(cholesky)/cholesky | solution.py:90
  309.9 11.7 %cholesky.257 = f32[128,128]{1,0:T(8,128)S(1)} custom-call(f32[128,128]{1,0:T(8,128)S(1)} %slice_subtract_fusion), custom_call_target="Cholesky" | custom-call | tf_op jit(solution)/shard_map/jit(cholesky)/cholesky | solution.py:90
  328.3 19.9 %custom-call.23 = f32[2,128,128]{1,2,0:T(8,128)S(1)} custom-call(f32[2,128,128]{2,1,0:T(8,128)S(1)} %get-tuple-element.29), custom_call_target="InvertDiagBlocksLowerTriangular" | custom-call | tf_op jit(solution)/shard_map/jit(_solve_triangular)/triangular_solve | solution.py:20
  (109 shorter events, 66.6 us)
Async XLA Ops:
  2.8 21.7 %all-to-all-start = ((f32[1,512,256]{2,0,1:T(1,128)}), f32[1,512,256]{2,0,1:T(1,128)S(1)}, u32[]{:S(2)}, u32[]{:S(2)}) async-start(f32[1,512,256]{2,0,1:T(1,128)} %reshape.142), calls=%async_computation | async-start | bytes 1048576 | tf_op jit(solution)/shard_map/all_to_all | solution.py:37
  28.2 29.3 %all-to-all-start.1 = ((f32[2,32,16,256]{3,2,0,1:T(8,128)}), f32[2,32,16,256]{3,2,0,1:T(8,128)S(1)}, u32[]{:S(2)}, u32[]{:S(2)}) async-start(f32[2,32,16,256]{3,2,0,1:T(8,128)} %copy.54), calls=%async_computation.1 | async-start | bytes 2097152 | tf_op jit(solution)/shard_map/all_to_all | solution.py:54
  63.2 5.6 %copy-start = (f32[1,512]{1,0:T(1,128)S(1)}, f32[1,512]{1,0:T(1,128)}, u32[]{:S(2)}) copy-start(f32[1,512]{1,0:T(1,128)} %param.6) | copy-start | bytes 6148
  138.6 18.8 %all-to-all-start.3 = ((f32[32,16,256]{2,1,0:T(8,128)}), f32[32,16,256]{2,1,0:T(8,128)S(1)}, u32[]{:S(2)}, u32[]{:S(2)}) async-start(f32[32,16,256]{2,1,0:T(8,128)} %copy.62), calls=%async_computation.3 | async-start | bytes 1048576 | tf_op jit(solution)/shard_map/all_to_all | solution.py:81
  158.5 65.7 %collective-permute-start = (f32[256,256]{0,1:T(8,128)S(1)}, f32[256,256]{0,1:T(8,128)S(1)}, u32[]{:S(2)}, u32[]{:S(2)}) collective-permute-start(f32[256,256]{0,1:T(8,128)S(1)} %fusion.3), channel_id=1, source_target_pairs={{0,1},{1,0},{2,3},{3,2},{4,5},{5,4},{6,7},{7,6},{8,9},{9,8},{10,11... | collective-permute-start | bytes 786440 | tf_op jit(solution)/shard_map/ppermute | solution.py:11
  224.2 63.2 %collective-permute-start.1 = (f32[256,256]{0,1:T(8,128)S(1)}, f32[256,256]{0,1:T(8,128)S(1)}, u32[]{:S(2)}, u32[]{:S(2)}) collective-permute-start(f32[256,256]{0,1:T(8,128)S(1)} %add.134), channel_id=1, source_target_pairs={{0,2},{1,3},{2,0},{3,1},{4,6},{5,7},{6,4},{7,5},{8,10},{9,11},{10,... | collective-permute-start | bytes 786440 | tf_op jit(solution)/shard_map/ppermute | solution.py:11
where the time goes:
time: 355 us; the launch traced here: 351 us
  other arithmetic  164 us (46%)
  matrix products  55.7 us (16%)
  waiting for transfers between devices  53.6 us (15%)
  blocking collectives  29.7 us (8%)
  local copies, waits for them, and re-layouts  22.8 us (6%)
  starting transfers between devices  19.5 us (5%)
  between operations  5.43 us (2%)
    another operation x7, other arithmetic, lower_solve(): return jax.scipy.linalg.solve_triangular(low, rhs, lower=True)  59.8 us
    dot_general x9, matrix products, matmul(): return jnp.dot(left, right, precision=lax.Precision.HIGHEST)  47.6 us
    another operation x7, other arithmetic, local(): pair_low = jnp.linalg.cholesky(pair_gram)  34.6 us
    another operation x7, other arithmetic, local(): leaf_low = jnp.linalg.cholesky(leaf_gram)  34.6 us
    another operation x7, other arithmetic, local(): group_low = jnp.linalg.cholesky(group_gram)  34.6 us
    all_to_all x1, blocking collectives, local(): lax.all_to_all(returned.reshape(2, 1, rows_dev, width), ('row', 'col'), s...  29.7 us
    all_to_all x1, waiting for transfers between devices, local(): lax.all_to_all(turned, ('row', 'col'), split_axis=1, concat_axis=2, tiled...  25 us
    all_to_all x1, waiting for transfers between devices, local(): lax.all_to_all(partial_sample, ('row', 'col'), split_axis=0, concat_axis=...  14.3 us
  transfers between devices with their start and end apart: 5, of which 3 were waited for; matrix products, arithmetic and copies ran while one was open for 35% of the time, Pallas kernels for 0%

commit v1 on v0

--- a/solution.py
+++ b/solution.py
@@ -3,6 +3,12 @@
 import jax.numpy as jnp
 from jax import lax
 from jax.sharding import PartitionSpec as P
+
+
+def make_the_entries(xin, where_dim, d0):
+    right_arr = jnp.stack(jnp.split(xin, lax.axis_size(("row", "col")), where_dim))
+    after = lax.all_to_all(right_arr, ("row", "col"), 0, 0)
+    return jnp.concatenate(after, d0)
 
 
 def partner(value, axis, distance):
@@ -34,9 +40,7 @@
     col_index = lax.axis_index("col")
     flat = lax.axis_index("row") * n_col + col_index
     highest = lax.Precision.HIGHEST
-    spread = lax.all_to_all(
-        probes.reshape(1, rows_dev, width), ("row", "col"), split_axis=1, concat_axis=0, tiled=True
-    )
+    spread = make_the_entries(probes.reshape(1, rows_dev, width), 1, 0)
     small_index = jnp.arange(devices, dtype=jnp.int32)
     cos_small, sin_small = circle(small_index[:, None] * small_index[None, :], devices)
     real_first = jnp.einsum("ka,abr->kbr", cos_small, spread, precision=highest)

time: 355 us -> 385 us (1.085)
  local copies, waits for them, and re-layouts: 22.8 us -> 51.5 us
    unnamed x12 -> x44, local copies, waits for them, and re-layouts: 3.45 us -> 33.7 us
  transfers between devices with their start and end apart: 5 -> 5, of which waited for: 3 -> 3; matrix products, arithmetic and copies ran while one was open for 35% -> 32% of each run, Pallas kernels for 0% -> 0%
where the time goes in v1:
time: 385 us; the launch traced here: 380 us
  other arithmetic  164 us (43%)
  matrix products  55.7 us (14%)
  waiting for transfers between devices  53.6 us (14%)
  local copies, waits for them, and re-layouts  51.5 us (13%)
  blocking collectives  29.7 us (8%)
  starting transfers between devices  19.5 us (5%)
  between operations  5.46 us (1%)
    another operation x7, other arithmetic, lower_solve(): return jax.scipy.linalg.solve_triangular(low, rhs, lower=True)  59.8 us
    dot_general x9, matrix products, matmul(): return jnp.dot(left, right, precision=lax.Precision.HIGHEST)  47.6 us
    another operation x7, other arithmetic, local(): leaf_low = jnp.linalg.cholesky(leaf_gram)  34.6 us
    another operation x7, other arithmetic, local(): pair_low = jnp.linalg.cholesky(pair_gram)  34.6 us
    another operation x7, other arithmetic, local(): group_low = jnp.linalg.cholesky(group_gram)  34.6 us
    unnamed x44, local copies, waits for them, and re-layouts  33.7 us
    all_to_all x1, blocking collectives, local(): lax.all_to_all(returned.reshape(2, 1, rows_dev, width), ('row', 'col'), s...  29.7 us
    all_to_all x1, waiting for transfers between devices, local(): lax.all_to_all(turned, ('row', 'col'), split_axis=1, concat_axis=2, tiled...  25 us
  transfers between devices with their start and end apart: 5, of which 3 were waited for; matrix products, arithmetic and copies ran while one was open for 32% of the time, Pallas kernels for 0%

profile of v1, /device:TPU:0, one launch (start us, length us, event | category | flops | bytes accessed | tf_op | source)
XLA Modules:
  0.0 379.7 jit_solution(10978442054884149369)
XLA Ops:
  31.6 7.3 %all-to-all-start = ((f32[32,1,16,256]{3,2,1,0:T(8,128)}), f32[32,1,16,256]{3,2,1,0:T(8,128)S(1)}, u32[]{:S(2)}, u32[]{:S(2)}) async-start(f32[32,1,16,256]{3,2,1,0:T(8,128)} %constant_dynamic-update-slice_fusion), calls=%async_computation | async-start | bytes 1048576 | tf_op jit(solution)/shard_map/all_to_all | solution.py:10
  39.0 14.2 %all-to-all-done = f32[32,1,16,256]{3,2,1,0:T(8,128)S(1)} async-done(((f32[32,1,16,256]{3,2,1,0:T(8,128)}), f32[32,1,16,256]{3,2,1,0:T(8,128)S(1)}, u32[]{:S(2)}, u32[]{:S(2)}) %all-to-all-start) | async-done | bytes 524320 | tf_op jit(solution)/shard_map/all_to_all | solution.py:10
  61.2 25.0 %all-to-all-done.1 = f32[2,32,16,256]{3,2,0,1:T(8,128)S(1)} async-done(((f32[2,32,16,256]{3,2,0,1:T(8,128)}), f32[2,32,16,256]{3,2,0,1:T(8,128)S(1)}, u32[]{:S(2)}, u32[]{:S(2)}) %all-to-all-start.1) | async-done | bytes 1048608 | tf_op jit(solution)/shard_map/all_to_all | solution.py:58
  91.9 5.6 %fusion.20 = f32[512,256]{1,0:T(8,128)S(1)} fusion(f32[512,256]{1,0:T(8,128)S(1)} %bitcast.321), kind=kOutput, calls=%fused_computation.46 | convolution fusion | flops 808976384 | bytes 1048576 | tf_op jit(solution)/shard_map/dot_general | solution.py:30
  97.5 5.6 %fusion = f32[512,256]{1,0:T(8,128)S(1)} fusion(f32[512,256]{1,0:T(8,128)S(1)} %fusion.24, f32[512,256]{1,0:T(8,128)S(1)} %bitcast.322, f32[512]{0:T(512)S(1)} %bitcast.323), kind=kOutput, calls=%fused_computation.13 | convolution fusion | flops 809238528 | bytes 1574912 | tf_op jit(solution)/shard_map/dot_general | solution.py:30
  103.2 5.6 %fusion.1 = f32[512,256]{1,0:T(8,128)S(1)} fusion(f32[512,256]{1,0:T(8,128)S(1)} %fusion.20, f32[512,256]{1,0:T(8,128)S(1)} %bitcast.320, f32[512]{0:T(512)S(1)} %bitcast.324), kind=kOutput, calls=%fused_computation.14 | convolution fusion | flops 809238528 | bytes 1574912 | tf_op jit(solution)/shard_map/dot_general | solution.py:30
  108.8 5.6 %fusion.18 = f32[512,256]{1,0:T(8,128)S(1)} fusion(f32[512,256]{1,0:T(8,128)S(1)} %fusion.1), kind=kOutput, calls=%fused_computation.45 | convolution fusion | flops 808976384 | bytes 1048576 | tf_op jit(solution)/shard_map/dot_general | solution.py:30
  114.4 5.6 %fusion.22 = f32[512,256]{1,0:T(8,128)S(1)} fusion(f32[512,256]{1,0:T(8,128)S(1)} %fusion), kind=kOutput, calls=%fused_computation.47 | convolution fusion | flops 808976384 | bytes 1048576 | tf_op jit(solution)/shard_map/dot_general | solution.py:30
  120.1 5.6 %convolution_add_fusion = f32[512,256]{1,0:T(8,128)S(1)} fusion(f32[512,256]{1,0:T(8,128)S(1)} %fusion.18, f32[512,256]{1,0:T(8,128)S(1)} %fusion), kind=kOutput, calls=%fused_computation.9 | convolution fusion | flops 809107456 | bytes 1572864 | tf_op jit(solution)/shard_map/dot_general | solution.py:30
  125.7 7.2 %subtract_bitcast_fusion = (f32[1,512,256]{2,1,0:T(8,128)S(1)}, f32[1,512,256]{2,1,0:T(8,128)S(1)}) fusion(f32[512,256]{1,0:T(8,128)S(1)} %convolution_add_fusion, f32[512]{0:T(512)S(1)} %get-tuple-element.108, f32[512]{0:T(512)S(1)} %get-tuple-element.109, f32[512,256]{1,0:T(8,128)S(1)} %fusion.22, f32[512,256]{1,0:T(8,128)S(1)} %fusion.1), kind=kOutput, calls=%fused_computation.40 | convolution fusion | flops 809893888 | bytes 2625536 | tf_op jit(solution)/shard_map/dot_general | solution.py:30
  133.8 29.7 %all_to_all.32 = f32[2,1,512,256]{3,0,1,2:T(2,128)S(1)} all-to-all(f32[2,1,512,256]{3,0,1,2:T(2,128)S(1)} %copy.53), channel_id=1, replica_groups=mesh['row'=8,'col'=4] {'row','col'}, dimensions={2} | all-to-all | bytes 2097152 | tf_op jit(solution)/shard_map/all_to_all | solution.py:74
  171.8 14.3 %all-to-all-done.3 = f32[32,16,256]{2,1,0:T(8,128)S(1)} async-done(((f32[32,16,256]{2,1,0:T(8,128)}), f32[32,16,256]{2,1,0:T(8,128)S(1)}, u32[]{:S(2)}, u32[]{:S(2)}) %all-to-all-start.3) | async-done | bytes 524320 | tf_op jit(solution)/shard_map/all_to_all | solution.py:85
  190.0 11.7 %cholesky.172 = f32[128,128]{1,0:T(8,128)S(1)} custom-call(f32[128,128]{1,0:T(8,128)S(1)} %cholesky.270), custom_call_target="Cholesky" | custom-call | tf_op jit(solution)/shard_map/jit(cholesky)/cholesky | solution.py:88
  201.7 9.8 %custom-call.19 = f32[1,128,128]{1,2,0:T(8,128)S(1)} custom-call(f32[1,128,128]{2,1,0:T(8,128)S(1)} %get-tuple-element.101), custom_call_target="InvertDiagBlocksLowerTriangular" | custom-call | tf_op jit(solution)/shard_map/jit(cholesky)/cholesky | solution.py:88
  212.0 11.7 %cholesky.189 = f32[128,128]{1,0:T(8,128)S(1)} custom-call(f32[128,128]{1,0:T(8,128)S(1)} %convolution_subtract_fusion.6), custom_call_target="Cholesky" | custom-call | tf_op jit(solution)/shard_map/jit(cholesky)/cholesky | solution.py:88
  230.5 19.8 %custom-call.15 = f32[2,128,128]{1,2,0:T(8,128)S(1)} custom-call(f32[2,128,128]{2,1,0:T(8,128)S(1)} %get-tuple-element.21), custom_call_target="InvertDiagBlocksLowerTriangular" | custom-call | tf_op jit(solution)/shard_map/jit(_solve_triangular)/triangular_solve | solution.py:26
  254.0 11.7 %cholesky.206 = f32[128,128]{1,0:T(8,128)S(1)} custom-call(f32[128,128]{1,0:T(8,128)S(1)} %cholesky.273), custom_call_target="Cholesky" | custom-call | tf_op jit(solution)/shard_map/jit(cholesky)/cholesky | solution.py:92
  265.7 9.8 %custom-call.20 = f32[1,128,128]{1,2,0:T(8,128)S(1)} custom-call(f32[1,128,128]{2,1,0:T(8,128)S(1)} %get-tuple-element.97), custom_call_target="InvertDiagBlocksLowerTriangular" | custom-call | tf_op jit(solution)/shard_map/jit(cholesky)/cholesky | solution.py:92
  276.0 11.7 %cholesky.223 = f32[128,128]{1,0:T(8,128)S(1)} custom-call(f32[128,128]{1,0:T(8,128)S(1)} %slice_subtract_fusion.1), custom_call_target="Cholesky" | custom-call | tf_op jit(solution)/shard_map/jit(cholesky)/cholesky | solution.py:92
  294.4 19.9 %custom-call.21 = f32[2,128,128]{1,2,0:T(8,128)S(1)} custom-call(f32[2,128,128]{2,1,0:T(8,128)S(1)} %get-tuple-element.28), custom_call_target="InvertDiagBlocksLowerTriangular" | custom-call | tf_op jit(solution)/shard_map/jit(_solve_triangular)/triangular_solve | solution.py:26
  316.3 11.7 %cholesky.240 = f32[128,128]{1,0:T(8,128)S(1)} custom-call(f32[128,128]{1,0:T(8,128)S(1)} %cholesky.276), custom_call_target="Cholesky" | custom-call | tf_op jit(solution)/shard_map/jit(cholesky)/cholesky | solution.py:94
  328.1 9.8 %custom-call.22 = f32[1,128,128]{1,2,0:T(8,128)S(1)} custom-call(f32[1,128,128]{2,1,0:T(8,128)S(1)} %get-tuple-element.93), custom_call_target="InvertDiagBlocksLowerTriangular" | custom-call | tf_op jit(solution)/shard_map/jit(cholesky)/cholesky | solution.py:94
  338.6 11.7 %cholesky.257 = f32[128,128]{1,0:T(8,128)S(1)} custom-call(f32[128,128]{1,0:T(8,128)S(1)} %slice_subtract_fusion), custom_call_target="Cholesky" | custom-call | tf_op jit(solution)/shard_map/jit(cholesky)/cholesky | solution.py:94
  357.0 19.9 %custom-call.23 = f32[2,128,128]{1,2,0:T(8,128)S(1)} custom-call(f32[2,128,128]{2,1,0:T(8,128)S(1)} %get-tuple-element.29), custom_call_target="InvertDiagBlocksLowerTriangular" | custom-call | tf_op jit(solution)/shard_map/jit(_solve_triangular)/triangular_solve | solution.py:26
  (141 shorter events, 95.3 us)
Async XLA Ops:
  0.6 21.2 %copy-start = (f32[512,256]{1,0:T(8,128)S(1)}, f32[512,256]{1,0:T(8,128)}, u32[]{:S(2)}) copy-start(f32[512,256]{1,0:T(8,128)} %param.5) | copy-start | bytes 1572868
  31.6 21.7 %all-to-all-start = ((f32[32,1,16,256]{3,2,1,0:T(8,128)}), f32[32,1,16,256]{3,2,1,0:T(8,128)S(1)}, u32[]{:S(2)}, u32[]{:S(2)}) async-start(f32[32,1,16,256]{3,2,1,0:T(8,128)} %constant_dynamic-update-slice_fusion), calls=%async_computation | async-start | bytes 1048576 | tf_op jit(solution)/shard_map/all_to_all | solution.py:10
  56.9 29.3 %all-to-all-start.1 = ((f32[2,32,16,256]{3,2,0,1:T(8,128)}), f32[2,32,16,256]{3,2,0,1:T(8,128)S(1)}, u32[]{:S(2)}, u32[]{:S(2)}) async-start(f32[2,32,16,256]{3,2,0,1:T(8,128)} %copy.50), calls=%async_computation.1 | async-start | bytes 2097152 | tf_op jit(solution)/shard_map/all_to_all | solution.py:58
  91.9 5.6 %copy-start.1 = (f32[1,512]{1,0:T(1,128)S(1)}, f32[1,512]{1,0:T(1,128)}, u32[]{:S(2)}) copy-start(f32[1,512]{1,0:T(1,128)} %param.6) | copy-start | bytes 6148
  167.3 18.8 %all-to-all-start.3 = ((f32[32,16,256]{2,1,0:T(8,128)}), f32[32,16,256]{2,1,0:T(8,128)S(1)}, u32[]{:S(2)}, u32[]{:S(2)}) async-start(f32[32,16,256]{2,1,0:T(8,128)} %copy.58), calls=%async_computation.3 | async-start | bytes 1048576 | tf_op jit(solution)/shard_map/all_to_all | solution.py:85
  187.2 65.7 %collective-permute-start = (f32[256,256]{0,1:T(8,128)S(1)}, f32[256,256]{0,1:T(8,128)S(1)}, u32[]{:S(2)}, u32[]{:S(2)}) collective-permute-start(f32[256,256]{0,1:T(8,128)S(1)} %fusion.3), channel_id=1, source_target_pairs={{0,1},{1,0},{2,3},{3,2},{4,5},{5,4},{6,7},{7,6},{8,9},{9,8},{10,11... | collective-permute-start | bytes 786440 | tf_op jit(solution)/shard_map/ppermute | solution.py:17
  252.9 63.2 %collective-permute-start.1 = (f32[256,256]{0,1:T(8,128)S(1)}, f32[256,256]{0,1:T(8,128)S(1)}, u32[]{:S(2)}, u32[]{:S(2)}) collective-permute-start(f32[256,256]{0,1:T(8,128)S(1)} %add.134), channel_id=1, source_target_pairs={{0,2},{1,3},{2,0},{3,1},{4,6},{5,7},{6,4},{7,5},{8,10},{9,11},{10,... | collective-permute-start | bytes 786440 | tf_op jit(solution)/shard_map/ppermute | solution.py:17
